TPU v7x, 32 devices: a whole 2x2x4 slice. The times are simulated.
32 devices in a mesh: samples: 4 (over y, x), channel: 4 (over z), spatial: 2 (over core).
Axes of the slice: x: 2, y: 2, z: 4, core: 2. Of those that a mesh axis runs over, the one named last changes fastest.
Arguments:
- features: bfloat16 [512, 4, 2, 1024], P('channel', 'samples', 'spatial'), may hold values from -6 to 6
- conv_one: bfloat16 [27, 512, 512], P(None, 'channel'), may hold values from -0.0625 to 0.0625
- conv_two: bfloat16 [27, 512, 512], P(None, 'channel'), may hold values from -0.0625 to 0.0625
- cotangent: bfloat16 [512, 4, 2, 1024], P('channel', 'samples', 'spatial'), may hold values from -6 to 6
Outputs:
- mixed_out: bfloat16 [512, 4, 2, 1024], P('channel', 'samples', 'spatial')
- input_grad: bfloat16 [512, 4, 2, 1024], P('channel', 'samples', 'spatial')
- grad_one: float32 [27, 512, 512], P(None, 'channel')
- grad_two: float32 [27, 512, 512], P(None, 'channel')
All inputs are finite; a program needn't handle non-finite values.
Results may differ from a plain program's by a relative error of at most 0.017.
Values may be sent and summed in bfloat16 or wider, within the bound.
A program may use at most 128 MiB of HBM per device.

v0:
```python
import jax
import jax.numpy as jnp
from jax import lax
from jax.sharding import PartitionSpec as P

SIDE = 32


def with_halo(shard, sides, width):
    for axis, dim in sides:
        size, length = (lax.axis_size(axis), shard.shape[dim])
        up = [(i, (i + 1) % size) for i in range(size - 1)]
        down = [(j, i) for i, j in up]
        last = lax.slice_in_dim(shard, length - width, length, axis=dim)
        first = lax.slice_in_dim(shard, 0, width, axis=dim)
        before = lax.ppermute(last, axis, up)
        after = lax.ppermute(first, axis, down)
        shard = jnp.concatenate([before, shard, after], axis=dim)
    return shard


def to_grid(values):
    return values.reshape(values.shape[0], values.shape[1], values.shape[2], SIDE, SIDE)


def to_flat(values):
    return values.reshape(values.shape[0], values.shape[1], values.shape[2], SIDE * SIDE)


def as_taps(kernel):
    return kernel.reshape(3, 3, 3, kernel.shape[1], kernel.shape[2])


def forward_conv(source, kernel, rhs_spec):
    return lax.conv_general_dilated(
        source,
        as_taps(kernel),
        (1, 1, 1),
        [(0, 0), (1, 1), (1, 1)],
        dimension_numbers=("CNDHW", rhs_spec, "CNDHW"),
        preferred_element_type=jnp.float32,
    )


def data_grad(source, kernel, rhs_spec):
    flipped = as_taps(kernel)[::-1, ::-1, ::-1]
    return lax.conv_general_dilated(
        source,
        flipped,
        (1, 1, 1),
        [(0, 0), (1, 1), (1, 1)],
        dimension_numbers=("CNDHW", rhs_spec, "CNDHW"),
        preferred_element_type=jnp.float32,
    )


def weight_grad(padded, upstream, out_spec):
    result = lax.conv_general_dilated(
        padded,
        upstream,
        (1, 1, 1),
        [(0, 0), (0, 0), (0, 0)],
        dimension_numbers=("NCDHW", "OIDHW", out_spec),
        preferred_element_type=jnp.float32,
    )
    return result.reshape(27, result.shape[3], result.shape[4])


def pad_plane(values):
    return jnp.pad(values, ((0, 0), (0, 0), (0, 0), (1, 1), (1, 1)))


def body(features, conv_one, conv_two, cotangent):
    rims_x = with_halo(features, (("spatial", 2),), 1)
    whole_x = lax.all_gather(rims_x, "channel", axis=0, tiled=True)
    pre_act = forward_conv(to_grid(whole_x), conv_one, "DHWOI")
    hidden = jax.nn.silu(pre_act).astype(jnp.bfloat16)
    rims_h = with_halo(to_flat(hidden), (("spatial", 2),), 1)
    grid_h = to_grid(rims_h)
    weight_part = conv_two
    mixed_out = lax.psum_scatter(
        to_flat(forward_conv(grid_h, weight_part, "DHWIO")),
        "channel",
        scatter_dimension=0,
        tiled=True,
    ).astype(jnp.bfloat16)
    rims_c = with_halo(cotangent, (("spatial", 2),), 1)
    whole_c = to_grid(lax.all_gather(rims_c, "channel", axis=0, tiled=True))
    hidden_grad = data_grad(whole_c, conv_two, "DHWOI")
    sigmoid_v = jax.nn.sigmoid(pre_act)
    act_grad = (hidden_grad * sigmoid_v * (1.0 + pre_act * (1.0 - sigmoid_v))).astype(jnp.bfloat16)
    rims_g = with_halo(to_flat(act_grad), (("spatial", 2),), 1)
    grid_g = to_grid(rims_g)
    weight_part = conv_one
    input_grad = lax.psum_scatter(
        to_flat(data_grad(grid_g, weight_part, "DHWIO")).astype(jnp.bfloat16),
        "channel",
        scatter_dimension=0,
        tiled=True,
    )
    local_two = weight_grad(pad_plane(grid_h), whole_c[:, :, 1:-1], "DHWNC")
    local_one = weight_grad(pad_plane(to_grid(whole_x)), act_grad, "DHWCN")
    grad_one, grad_two = (
        lax.psum(local_one.astype(jnp.bfloat16), ("samples", "spatial")).astype(jnp.float32),
        lax.psum(local_two.astype(jnp.bfloat16), ("samples", "spatial")).astype(jnp.float32),
    )
    return (mixed_out, input_grad, grad_one, grad_two)


def solution(mesh):
    placed = (
        P("channel", "samples", "spatial", None),
        P(None, "channel", None),
        P(None, "channel", None),
        P("channel", "samples", "spatial", None),
    )
    return jax.shard_map(
        body,
        mesh=mesh,
        in_specs=placed,
        out_specs=(
            P("channel", "samples", "spatial", None),
            P("channel", "samples", "spatial", None),
            P(None, "channel", None),
            P(None, "channel", None),
        ),
        check_vma=False,
    )
```

profile of v0, /device:TPU:0, one launch (start us, length us, event | category | flops | bytes accessed | tf_op | source)
XLA Modules:
  0.0 412.6 jit_solution(8968176364339753036)
XLA Ops:
  9.2 2.4 collective-permute-start
  12.9 2.3 collective-permute-done.1
  26.7 56.1 %all-gather.3.cloned.1.call-done = bf16[512,1,3,1024]{0,3,2,1:T(8,128)(2,1)} async-done(((bf16[128,1,3,1024]{0,3,2,1:T(8,128)(2,1)}), bf16[512,1,3,1024]{0,3,2,1:T(8,128)(2,1)}) %all-gather.3.cloned.1.call-update) | async-done | bytes 3145744 | tf_op jit(solution)/shard_map/all_gather | solution.py:75
  82.8 3.6 copy.144
  90.7 10.3 %multiply_convert_fusion = (bf16[1,32,8,5,128]{4,2,3,1,0:T(8,128)(2,1)S(1)}, f32[1,32,8,5,128]{4,2,3,1,0:T(8,128)}) fusion(bf16[3,3,3,128,512]{4,3,2,1,0:T(8,128)(2,1)S(1)} %bitcast.81, bf16[512,3,32,1,7,2]{0,4,5,2,1,3:T(8,128)(2,1)S(1)} %slice.16, bf16[512,3,32,1,8,5]{0,4,5,2,1,3:T(8,128)(2,1)S(1)} %copy.96, pred[8,5]{0,1:T(8,128)(4,1)S(1)} %copy-done.15), kind=kOutput, calls=%fused_computation.63 | convolution fusion | flops 4452974592 | bytes 9830440 | tf_op jit(solution)/shard_map/conv_general_dilated | solution.py:35
  104.4 4.6 %collective-permute-start.2 = (bf16[128,1,1,1024]{0,3,2,1:T(8,128)(2,1)}, bf16[128,1,1,1024]{0,3,2,1:T(8,128)(2,1)}, u32[]{:S(2)}, u32[]{:S(2)}) collective-permute-start(bf16[128,1,1,1024]{0,3,2,1:T(8,128)(2,1)} %bitcast.42), channel_id=1, source_target_pairs={{0,1},{2,3},{4,5},{6,7},{8,9},{10,11},{12,13},{14,15},{16,17},{18,... | collective-permute-start | bytes 786440 | tf_op jit(solution)/shard_map/ppermute | solution.py:16
  110.3 3.5 fusion.83
  113.8 32.2 %all-gather.5.cloned.1.call-done = bf16[512,1,3,1024]{0,3,2,1:T(8,128)(2,1)} async-done(((bf16[128,1,3,1024]{0,3,2,1:T(8,128)(2,1)}), bf16[512,1,3,1024]{0,3,2,1:T(8,128)(2,1)}) %all-gather.5.cloned.1.call-update) | async-done | bytes 3145744 | tf_op jit(solution)/shard_map/all_gather | solution.py:88
  145.9 3.6 copy.147
  152.9 9.7 %fusion.57 = bf16[1,32,8,5,128]{4,2,3,1,0:T(8,128)(2,1)S(1)} fusion(bf16[3,3,3,128,512]{4,3,2,1,0:T(8,128)(2,1)S(1)} %bitcast.105, bf16[512,3,32,1,7,2]{0,4,5,2,1,3:T(8,128)(2,1)S(1)} %slice.20, bf16[512,3,32,1,8,5]{0,4,5,2,1,3:T(8,128)(2,1)S(1)} %copy.111, f32[1,32,8,5,128]{4,2,3,1,0:T(8,128)S(1)} %copy-done.17, pred[8,5]{0,1:T(8,128)(4,1)S(1)} %copy-done.15), kind=kOutput, calls=%fused_computation.54 | convolution fusion | flops 4453629952 | bytes 9830440 | tf_op jit(solution)/shard_map/conv_general_dilated | solution.py:47
  175.1 15.5 %fusion.32 = bf16[3,3,3,128,512,1]{3,4,2,5,1,0:T(8,128)(2,1)} fusion(bf16[512,3,32,8,5,1]{0,3,5,4,2,1:T(8,128)(2,1)S(1)} %get-tuple-element.26, bf16[512,3,32,8,5,1]{0,3,5,4,2,1:T(8,128)(2,1)S(1)} %copy.126, bf16[512,3,32,8,5,1]{0,3,5,4,2,1:T(8,128)(2,1)S(1)} %get-tuple-element.27, bf16[1,32,8,5,128]{4,2,3,1,0:T(8,128)(2,1)S(1)} %fusion.57, ...), kind=kOutput, calls=%fused_computation.36 | convolution fusion | flops 4472799232 | bytes 15663144 | tf_op jit(solution)/shard_map/conv_general_dilated | solution.py:58
  190.5 5.9 %copy.128 = bf16[27,128,512]{2,1,0:T(8,128)(2,1)} copy(bf16[27,128,512]{1,2,0:T(8,128)(2,1)} %bitcast.99) | data formatting | bytes 7077888 | tf_op jit(solution)/shard_map/convert_element_type | solution.py:104
  196.4 2.4 slice.28
  198.8 2.3 copy.100
  201.1 2.3 copy.99
  206.3 4.9 %select_convert_fusion = bf16[1,32,8,5,512]{4,2,3,1,0:T(8,128)(2,1)S(1)} fusion(bf16[3,3,3,128,512]{4,3,2,1,0:T(8,128)(2,1)S(1)} %bitcast.82, bf16[128,3,32,1,7,2]{0,4,5,2,1,3:T(8,128)(2,1)S(1)} %slice.22, bf16[128,3,32,1,8,5]{0,4,5,2,1,3:T(8,128)(2,1)S(1)} %copy.117, pred[8,5]{0,1:T(8,128)(4,1)S(1)} %copy-done.15), kind=kOutput, calls=%fused_computation.34 | convolution fusion | flops 4440915968 | bytes 6176808 | tf_op jit(solution)/shard_map/conv_general_dilated | solution.py:47
  213.7 4.4 %pad_maximum_fusion = bf16[128,1,3,32,32]{0,1,4,3,2:T(2,128)(2,1)S(1)} fusion(bf16[128,1,1,32,32]{0,1,4,3,2:T(2,128)(2,1)} %copy.100, bf16[128,1,1,32,32]{0,1,4,3,2:T(2,128)(2,1)S(1)} %bitcast.93, bf16[128,1,1,32,32]{0,1,4,3,2:T(2,128)(2,1)} %copy.99), kind=kLoop, calls=%fused_computation.40 | loop fusion | flops 786432 | bytes 1572864 | tf_op jit(solution)/shard_map/concatenate | solution.py:18
  218.1 20.5 %convolution_convert_fusion = bf16[3,3,3,128,512]{4,3,2,1,0:T(8,128)(2,1)} fusion(bf16[128,1,3,32,32]{0,1,4,3,2:T(2,128)(2,1)S(1)} %pad_maximum_fusion, bf16[512,1,1,32,32]{0,4,3,2,1:T(8,128)(2,1)} %slice.28), kind=kOutput, calls=%fused_computation.35 | convolution fusion | flops 3476226048 | bytes 5373952 | tf_op jit(solution)/shard_map/conv_general_dilated | solution.py:58
  240.9 5.0 %convolution_select_fusion = f32[1,32,8,5,512]{4,2,3,1,0:T(8,128)S(1)} fusion(bf16[3,3,3,128,512]{4,3,2,1,0:T(8,128)(2,1)S(1)} %bitcast.106, bf16[128,3,32,1,7,2]{0,4,5,2,1,3:T(8,128)(2,1)S(1)} %slice.18, bf16[128,3,32,1,8,5]{0,4,5,2,1,3:T(8,128)(2,1)S(1)} %copy.103, pred[8,5]{0,1:T(8,128)(4,1)S(1)} %copy-done.16), kind=kOutput, calls=%fused_computation.39 | convolution fusion | flops 4440260608 | bytes 7487528 | tf_op jit(solution)/shard_map/conv_general_dilated | solution.py:35
  247.6 2.6 copy.105
  252.2 103.9 %all-reduce.3.cloned.1.call-done = (bf16[27,128,512]{2,1,0:T(8,128)(2,1)}, bf16[27,128,512]{2,1,0:T(8,128)(2,1)}) async-done(((bf16[27,128,512]{2,1,0:T(8,128)(2,1)}, bf16[27,128,512]{2,1,0:T(8,128)(2,1)}), (bf16[27,128,512]{2,1,0:T(8,128)(2,1)}, bf16[27,128,512]{2,1,0:T(8,128)(2,1)})) %all-reduce.3.cloned.1.call-update) | async-done | bytes 7077904 | tf_op jit(solution)/shard_map/psum | solution.py:104
  356.2 6.1 %convert_element_type.52 = f32[27,128,512]{2,1,0:T(8,128)} convert(bf16[27,128,512]{2,1,0:T(8,128)(2,1)} %get-tuple-element.16) | non-fusion elementwise | flops 1769472 | bytes 10616832 | tf_op jit(solution)/shard_map/convert_element_type | solution.py:104
  362.2 4.0 convert_element_type.55
  366.2 35.9 %reduce-scatter.5.cloned.1.call-done = f32[128,1,1,1024]{0,3,2,1:T(8,128)} async-done(((f32[512,1,1,1024]{0,3,2,1:T(8,128)}), f32[128,1,1,1024]{0,3,2,1:T(8,128)}) %reduce-scatter.5.cloned.1.call-update) | async-done | bytes 524304 | tf_op jit(solution)/shard_map/reduce_scatter | solution.py:81
  (105 shorter events, 54.0 us)
Async XLA Ops:
  7.2 83.5 %copy-start = (bf16[27,128,512]{2,1,0:T(8,128)(2,1)S(1)}, bf16[27,128,512]{2,1,0:T(8,128)(2,1)}, u32[]{:S(2)}) copy-start(bf16[27,128,512]{2,1,0:T(8,128)(2,1)} %param.5) | copy-start | bytes 10616836
  7.2 75.6 %all-gather.3.cloned.1.call-start = ((), (), s32[]{:S(2)}) async-start(), calls=%async_computation.2 | async-start | bytes 3932160 | tf_op jit(solution)/shard_map/all_gather | solution.py:75
  9.2 3.7 collective-permute-start
  11.6 3.6 collective-permute-start.1
  17.2 128.8 %all-gather.5.cloned.1.call-start = ((), (), s32[]{:S(2)}) async-start(), calls=%async_computation.4 | async-start | bytes 3932160 | tf_op jit(solution)/shard_map/all_gather | solution.py:88
  19.0 3.4 collective-permute-start.4
  21.1 3.6 collective-permute-start.5
  26.6 223.6 %reduce-scatter.7.cloned.1.call-start = ((), (), s32[]{:S(2)}) async-start(), calls=%async_computation.5 | async-start | bytes 1310720
  88.0 22.3 %copy-start.2 = (bf16[512,3,32,1,40]{0,2,4,1,3:T(8,128)(2,1)}, bf16[512,3,32,1,40]{0,2,4,1,3:T(8,128)(2,1)S(1)}, u32[]{:S(2)}) copy-start(bf16[512,3,32,1,40]{0,2,4,1,3:T(8,128)(2,1)S(1)} %get-tuple-element.22) | copy-start | bytes 11796484
  88.0 2.7 copy-start.15
  103.1 95.7 %collective-permute-start.3 = (bf16[128,1,1,1024]{0,3,2,1:T(8,128)(2,1)}, bf16[128,1,1,1024]{0,3,2,1:T(8,128)(2,1)}, u32[]{:S(2)}, u32[]{:S(2)}) collective-permute-start(bf16[128,1,1,1024]{0,3,2,1:T(8,128)(2,1)} %bitcast.42), channel_id=1, source_target_pairs={{1,0},{3,2},{5,4},{7,6},{9,8},{11,10},{13,12},{15,14},{17,16},{19,... | collective-permute-start | bytes 786440 | tf_op jit(solution)/shard_map/ppermute | solution.py:17
  104.4 96.7 %collective-permute-start.2 = (bf16[128,1,1,1024]{0,3,2,1:T(8,128)(2,1)}, bf16[128,1,1,1024]{0,3,2,1:T(8,128)(2,1)}, u32[]{:S(2)}, u32[]{:S(2)}) collective-permute-start(bf16[128,1,1,1024]{0,3,2,1:T(8,128)(2,1)} %bitcast.42), channel_id=1, source_target_pairs={{0,1},{2,3},{4,5},{6,7},{8,9},{10,11},{12,13},{14,15},{16,17},{18,... | collective-permute-start | bytes 786440 | tf_op jit(solution)/shard_map/ppermute | solution.py:16
  150.2 2.7 copy-start.13
  150.2 2.7 copy-start.17
  152.9 14.1 %copy-start.5 = (bf16[512,3,32,1,8,4]{0,2,5,4,1,3:T(8,128)(2,1)S(1)}, bf16[512,3,32,1,8,4]{0,2,5,4,1,3:T(8,128)(2,1)}, u32[]{:S(2)}) copy-start(bf16[512,3,32,1,8,4]{0,2,5,4,1,3:T(8,128)(2,1)} %get-tuple-element.18) | copy-start | bytes 9437188
  162.7 4.3 %copy-start.11 = (bf16[128,1,1,32,32]{0,3,4,1,2:T(8,128)(2,1)}, bf16[128,1,1,32,32]{0,3,4,1,2:T(8,128)(2,1)S(1)}, u32[]{:S(2)}) copy-start(bf16[128,1,1,32,32]{0,3,4,1,2:T(8,128)(2,1)S(1)} %slice_bitcast_fusion.2) | copy-start | bytes 786436
  162.7 6.0 %copy-start.4 = (bf16[512,3,32,1,8,4]{0,2,5,4,1,3:T(8,128)(2,1)S(1)}, bf16[512,3,32,1,8,4]{0,2,5,4,1,3:T(8,128)(2,1)}, u32[]{:S(2)}) copy-start(bf16[512,3,32,1,8,4]{0,2,5,4,1,3:T(8,128)(2,1)} %get-tuple-element.19) | copy-start | bytes 9437188
  163.5 40.0 %collective-permute-start.6 = (bf16[128,1,1,1024]{0,3,2,1:T(8,128)(2,1)}, bf16[128,1,1,1024]{0,3,2,1:T(8,128)(2,1)}, u32[]{:S(2)}, u32[]{:S(2)}) collective-permute-start(bf16[128,1,1,1024]{0,3,2,1:T(8,128)(2,1)} %bitcast.20), channel_id=1, source_target_pairs={{0,1},{2,3},{4,5},{6,7},{8,9},{10,11},{12,13},{14,15},{16,17},{18,... | collective-permute-start | bytes 786440 | tf_op jit(solution)/shard_map/ppermute | solution.py:16
  165.6 38.9 %collective-permute-start.7 = (bf16[128,1,1,1024]{0,3,2,1:T(8,128)(2,1)}, bf16[128,1,1,1024]{0,3,2,1:T(8,128)(2,1)}, u32[]{:S(2)}, u32[]{:S(2)}) collective-permute-start(bf16[128,1,1,1024]{0,3,2,1:T(8,128)(2,1)} %bitcast.20), channel_id=1, source_target_pairs={{1,0},{3,2},{5,4},{7,6},{9,8},{11,10},{13,12},{15,14},{17,16},{19,... | collective-permute-start | bytes 786440 | tf_op jit(solution)/shard_map/ppermute | solution.py:17
  196.4 9.2 %copy-start.12 = (bf16[128,1,1,32,32]{0,3,4,1,2:T(8,128)(2,1)S(1)}, bf16[128,1,1,32,32]{0,3,4,1,2:T(8,128)(2,1)}, u32[]{:S(2)}) copy-start(bf16[128,1,1,32,32]{0,3,4,1,2:T(8,128)(2,1)} %copy-done.11) | copy-start | bytes 786436
  213.7 142.5 %all-reduce.3.cloned.1.call-start = ((), (), s32[]{:S(2)}) async-start(), calls=%async_computation.6 | async-start | bytes 14155776 | tf_op jit(solution)/shard_map/psum | solution.py:104
  238.7 163.4 %reduce-scatter.5.cloned.1.call-start = ((), (), s32[]{:S(2)}) async-start(), calls=%async_computation.3 | async-start | bytes 2621440 | tf_op jit(solution)/shard_map/reduce_scatter | solution.py:81
  356.2 6.1 %copy-start.8 = (bf16[27,128,512]{2,1,0:T(8,128)(2,1)S(1)}, bf16[27,128,512]{2,1,0:T(8,128)(2,1)}, u32[]{:S(2)}) copy-start(bf16[27,128,512]{2,1,0:T(8,128)(2,1)} %get-tuple-element.17) | copy-start | bytes 10616836
  362.2 43.4 %copy-start.1 = (bf16[27,128,512]{2,1,0:T(8,128)(2,1)S(1)}, bf16[27,128,512]{2,1,0:T(8,128)(2,1)}, u32[]{:S(2)}) copy-start(bf16[27,128,512]{2,1,0:T(8,128)(2,1)} %param.5) | copy-start | bytes 10616836
  (7 other events, 13.6 us)
Sparse Core Ops, SparseCore 0:
  17.3 65.4 all-gather.2
  84.3 61.5 all-gather.4
  213.8 27.3 reduce-scatter.6
  245.0 111.0 all-reduce.2
  358.3 43.7 reduce-scatter.4
where the time goes:
time: 416 us; the launch traced here: 413 us
  waiting for transfers between devices  233 us (56%)
  matrix products  65.8 us (16%)
  local copies, waits for them, and re-layouts  61.1 us (15%)
  other arithmetic  21.6 us (5%)
  starting transfers between devices  16.5 us (4%)
  between operations  14.8 us (4%)
    psum x1, waiting for transfers between devices, body(): lax.psum(local_one.astype(jnp.bfloat16), ('samples', 'spatial'))  104 us
    all_gather x1, waiting for transfers between devices, body(): whole_x = lax.all_gather(rims_x, 'channel', axis=0, tiled=True)  56.1 us
    conv_general_dilated x2, matrix products, weight_grad(): lax.conv_general_dilated(padded, upstream, (1, 1, 1), [(0, 0), (0, 0), (0...  36 us
    reduce_scatter x1, waiting for transfers between devices, body(): lax.psum_scatter(to_flat(forward_conv(grid_h, weight_part, 'DHWIO')), 'ch...  35.9 us
    all_gather x1, waiting for transfers between devices, body(): whole_c = to_grid(lax.all_gather(rims_c, 'channel', axis=0, tiled=True))  32.2 us
    unnamed x52, local copies, waits for them, and re-layouts  24.2 us
    conv_general_dilated x2, matrix products, forward_conv(): lax.conv_general_dilated(source, as_taps(kernel), (1, 1, 1), [(0, 0), (1,...  15.2 us
    conv_general_dilated x2, matrix products, data_grad(): lax.conv_general_dilated(source, flipped, (1, 1, 1), [(0, 0), (1, 1), (1,...  14.6 us
  transfers between devices with their start and end apart: 13, of which 6 were waited for; matrix products, arithmetic and copies ran while one was open for 32% of the time, Pallas kernels for 0%

commit v1 on v0

--- a/solution.py
+++ b/solution.py
@@ -4,6 +4,27 @@
 from jax.sharding import PartitionSpec as P
 
 SIDE = 32
+
+
+def joined_along(parts, dim):
+    parts = jnp.moveaxis(parts, 0, dim)
+    lengths = parts.shape
+    return parts.reshape(*lengths[:dim], lengths[dim] * lengths[dim + 1], *lengths[dim + 2 :])
+
+
+def grow_blocks(x, axis):
+    size, position = (lax.axis_size(axis), lax.axis_index(axis))
+    parts, bit = (x[None], 1)
+    while bit < size:
+        other = lax.ppermute(parts, axis, [(i, i ^ bit) for i in range(size)])
+        low = position & bit == 0
+        parts = jnp.concatenate([jnp.where(low, parts, other), jnp.where(low, other, parts)])
+        bit *= 2
+    return parts
+
+
+def doubled_up(x, axis, dim):
+    return joined_along(grow_blocks(x, axis), dim)
 
 
 def with_halo(shard, sides, width):
@@ -85,7 +106,7 @@
         tiled=True,
     ).astype(jnp.bfloat16)
     rims_c = with_halo(cotangent, (("spatial", 2),), 1)
-    whole_c = to_grid(lax.all_gather(rims_c, "channel", axis=0, tiled=True))
+    whole_c = to_grid(doubled_up(rims_c, "channel", 0))
     hidden_grad = data_grad(whole_c, conv_two, "DHWOI")
     sigmoid_v = jax.nn.sigmoid(pre_act)
     act_grad = (hidden_grad * sigmoid_v * (1.0 + pre_act * (1.0 - sigmoid_v))).astype(jnp.bfloat16)

time: 416 us -> 506 us (1.22); the launches traced: 413 us -> 497 us
  waiting for transfers between devices: 233 us -> 276 us
  local copies, waits for them, and re-layouts: 61.1 us -> 87.8 us
  other arithmetic: 21.6 us -> 29.2 us
  starting transfers between devices: 16.5 us -> 22.1 us
    ppermute x0 -> x2, waiting for transfers between devices: none -> 132 us  [grow_blocks(): other = lax.ppermute(parts, axis, [(i, i ^ bit) for i in range(size)])]
    all_gather x1, waiting for transfers between devices: 56.1 us -> 0.01 us  [body(): whole_x = lax.all_gather(rims_x, 'channel', axis=0, tiled=True)]
    all_gather x1 -> x0, waiting for transfers between devices: 32.2 us -> none  [body(): whole_c = to_grid(lax.all_gather(rims_c, 'channel', axis=0, tiled=True))]
    another operation x0 -> x3, local copies, waits for them, and re-layouts: none -> 24.6 us  [to_grid(): values.reshape(values.shape[0], values.shape[1], values.shape[2], SIDE, S...]
    concatenate x0 -> x1, local copies, waits for them, and re-layouts: none -> 5.92 us  [grow_blocks(): jnp.concatenate([jnp.where(low, parts, other), jnp.where(low, other, part...]
    ppermute x0 -> x2, starting transfers between devices: none -> 5.24 us  [grow_blocks(): other = lax.ppermute(parts, axis, [(i, i ^ bit) for i in range(size)])]
    unnamed x52 -> x47, local copies, waits for them, and re-layouts: 24.2 us -> 25.1 us
  transfers between devices with their start and end apart: 13 -> 14, of which waited for: 6 -> 6; matrix products, arithmetic and copies ran while one was open for 32% -> 29% of each run, Pallas kernels for 0% -> 0%
where the time goes in v1:
time: 506 us; the launch traced here: 497 us
  waiting for transfers between devices  276 us (55%)
  local copies, waits for them, and re-layouts  87.8 us (17%)
  matrix products  67.2 us (13%)
  other arithmetic  29.2 us (6%)
  starting transfers between devices  22.1 us (4%)
  between operations  14.5 us (3%)
    ppermute x2, waiting for transfers between devices, grow_blocks(): other = lax.ppermute(parts, axis, [(i, i ^ bit) for i in range(size)])  132 us
    psum x1, waiting for transfers between devices, body(): lax.psum(local_one.astype(jnp.bfloat16), ('samples', 'spatial'))  104 us
    conv_general_dilated x2, matrix products, weight_grad(): lax.conv_general_dilated(padded, upstream, (1, 1, 1), [(0, 0), (0, 0), (0...  36.5 us
    reduce_scatter x1, waiting for transfers between devices, body(): lax.psum_scatter(to_flat(forward_conv(grid_h, weight_part, 'DHWIO')), 'ch...  35.9 us
    unnamed x47, local copies, waits for them, and re-layouts  25.1 us
    another operation x3, local copies, waits for them, and re-layouts, to_grid(): values.reshape(values.shape[0], values.shape[1], values.shape[2], SIDE, S...  24.6 us
    conv_general_dilated x2, matrix products, data_grad(): lax.conv_general_dilated(source, flipped, (1, 1, 1), [(0, 0), (1, 1), (1,...  16.3 us
    conv_general_dilated x2, matrix products, forward_conv(): lax.conv_general_dilated(source, as_taps(kernel), (1, 1, 1), [(0, 0), (1,...  14.4 us
  transfers between devices with their start and end apart: 14, of which 6 were waited for; matrix products, arithmetic and copies ran while one was open for 29% of the time, Pallas kernels for 0%

profile of v1, /device:TPU:0, one launch (start us, length us, event | category | flops | bytes accessed | tf_op | source)
XLA Modules:
  0.0 497.2 jit_solution(5834561605258486011)
XLA Ops:
  9.2 2.4 collective-permute-start
  24.9 2.4 collective-permute-start.6
  27.3 42.5 %collective-permute-done.6 = bf16[1,128,1,3,1024]{4,1,3,2,0:T(8,128)(2,1)} collective-permute-done((bf16[1,128,1,3,1024]{4,1,3,2,0:T(8,128)(2,1)}, bf16[1,128,1,3,1024]{4,1,3,2,0:T(8,128)(2,1)}, u32[]{:S(2)}, u32[]{:S(2)}) %collective-permute-start.6) | collective-permute-done | bytes 786464 | tf_op jit(solution)/shard_map/ppermute | solution.py:19
  73.5 2.8 collective-permute-start.7
  76.4 89.3 %collective-permute-done.7 = bf16[2,128,1,3,1024]{4,1,3,2,0:T(8,128)(2,1)} collective-permute-done((bf16[2,128,1,3,1024]{4,1,3,2,0:T(8,128)(2,1)}, bf16[2,128,1,3,1024]{4,1,3,2,0:T(8,128)(2,1)}, u32[]{:S(2)}, u32[]{:S(2)}) %collective-permute-start.7) | collective-permute-done | bytes 1572896 | tf_op jit(solution)/shard_map/ppermute | solution.py:19
  169.7 5.9 %copy.104 = bf16[4,128,1,3,1024]{1,0,4,3,2:T(4,128)(2,1)} copy(bf16[4,128,1,3,1024]{4,1,3,2,0:T(8,128)(2,1)} %pad_maximum_fusion) | data formatting | bytes 6291456 | tf_op jit(solution)/shard_map/concatenate | solution.py:21
  175.6 5.7 %reshape.112 = bf16[512,3,32,1,32]{0,4,2,1,3:T(8,128)(2,1)} reshape(bf16[4,128,1,3,1024]{1,0,4,3,2:T(4,128)(2,1)} %copy.104) | data formatting | bytes 6291456 | tf_op jit(solution)/shard_map/reshape;reshape | solution.py:44
  181.3 18.4 %reshape_reshape.4 = bf16[512,1,3,32,32]{0,1,4,3,2:T(2,128)(2,1)} reshape(bf16[4,128,1,3,1024]{1,0,4,3,2:T(4,128)(2,1)} %copy.104) | data formatting | bytes 6291456 | tf_op jit(solution)/shard_map/reshape;reshape | solution.py:44
  199.7 3.6 copy.143
  209.6 3.6 copy.140
  219.0 9.4 %multiply_convert_fusion = (bf16[1,32,8,5,128]{4,2,3,1,0:T(8,128)(2,1)S(1)}, f32[1,32,8,5,128]{4,2,3,1,0:T(8,128)S(1)}) fusion(bf16[3,3,3,128,512]{4,3,2,1,0:T(8,128)(2,1)S(1)} %bitcast.89, bf16[512,3,32,1,7,2]{0,4,5,2,1,3:T(8,128)(2,1)S(1)} %slice.16, bf16[512,3,32,1,8,5]{0,4,5,2,1,3:T(8,128)(2,1)S(1)} %copy.94, pred[8,5]{0,1:T(8,128)(4,1)S(1)} %copy-done.14), kind=kOutput, calls=%fused_computation.69 | convolution fusion | flops 4452974592 | bytes 9830440 | tf_op jit(solution)/shard_map/conv_general_dilated | solution.py:56
  234.4 11.4 %fusion.57 = bf16[1,32,8,5,128]{4,2,3,1,0:T(8,128)(2,1)S(1)} fusion(bf16[3,3,3,128,512]{4,3,2,1,0:T(8,128)(2,1)} %bitcast.111, bf16[512,3,32,1,7,2]{0,4,5,2,1,3:T(8,128)(2,1)S(1)} %copy-done.10, bf16[512,3,32,1,8,5]{0,4,5,2,1,3:T(8,128)(2,1)S(1)} %copy-done.3, f32[1,32,8,5,128]{4,2,3,1,0:T(8,128)S(1)} %get-tuple-element.29, pred[8,5]{0,1:T(8,128)(4,1)S(1)} %copy-done.14), kind=kOutput, calls=%fused_computation.58 | convolution fusion | flops 4453629952 | bytes 9830440 | tf_op jit(solution)/shard_map/conv_general_dilated | solution.py:68
  246.7 4.4 collective-permute-start.8
  260.5 15.5 %fusion.32 = bf16[3,3,3,128,512,1]{3,4,2,5,1,0:T(8,128)(2,1)} fusion(bf16[512,3,32,8,5,1]{0,3,5,4,2,1:T(8,128)(2,1)S(1)} %get-tuple-element.30, bf16[512,3,32,8,5,1]{0,3,5,4,2,1:T(8,128)(2,1)S(1)} %copy.122, bf16[512,3,32,8,5,1]{0,3,5,4,2,1:T(8,128)(2,1)S(1)} %get-tuple-element.31, bf16[1,32,8,5,128]{4,2,3,1,0:T(8,128)(2,1)S(1)} %fusion.57, ...), kind=kOutput, calls=%fused_computation.37 | convolution fusion | flops 4472799232 | bytes 15663144 | tf_op jit(solution)/shard_map/conv_general_dilated | solution.py:79
  276.0 6.2 %copy.124 = bf16[27,128,512]{2,1,0:T(8,128)(2,1)} copy(bf16[27,128,512]{1,2,0:T(8,128)(2,1)} %bitcast.105) | data formatting | bytes 7077888 | tf_op jit(solution)/shard_map/convert_element_type | solution.py:125
  290.6 4.9 select_convert_fusion
  298.0 4.3 pad_maximum_fusion.1
  302.4 21.1 %convolution_convert_fusion = bf16[3,3,3,128,512]{4,3,2,1,0:T(8,128)(2,1)} fusion(bf16[128,1,3,32,32]{0,1,4,3,2:T(2,128)(2,1)S(1)} %pad_maximum_fusion.1, bf16[512,1,3,32,32]{0,1,4,3,2:T(2,128)(2,1)} %reshape_reshape.4), kind=kOutput, calls=%fused_computation.36 | convolution fusion | flops 3476226048 | bytes 6422528 | tf_op jit(solution)/shard_map/conv_general_dilated | solution.py:79
  325.7 5.0 convolution_select_fusion
  332.4 2.6 copy.103
  337.1 103.9 %all-reduce.3.cloned.1.call-done = (bf16[27,128,512]{2,1,0:T(8,128)(2,1)}, bf16[27,128,512]{2,1,0:T(8,128)(2,1)}) async-done(((bf16[27,128,512]{2,1,0:T(8,128)(2,1)}, bf16[27,128,512]{2,1,0:T(8,128)(2,1)}), (bf16[27,128,512]{2,1,0:T(8,128)(2,1)}, bf16[27,128,512]{2,1,0:T(8,128)(2,1)})) %all-reduce.3.cloned.1.call-update) | async-done | bytes 7077904 | tf_op jit(solution)/shard_map/psum | solution.py:125
  440.9 6.1 %convert_element_type.52 = f32[27,128,512]{2,1,0:T(8,128)} convert(bf16[27,128,512]{2,1,0:T(8,128)(2,1)} %get-tuple-element.16) | non-fusion elementwise | flops 1769472 | bytes 10616832 | tf_op jit(solution)/shard_map/convert_element_type | solution.py:125
  447.0 4.0 convert_element_type.55
  451.0 35.9 %reduce-scatter.5.cloned.1.call-done = f32[128,1,1,1024]{0,3,2,1:T(8,128)} async-done(((f32[512,1,1,1024]{0,3,2,1:T(8,128)}), f32[128,1,1,1024]{0,3,2,1:T(8,128)}) %reduce-scatter.5.cloned.1.call-update) | async-done | bytes 524304 | tf_op jit(solution)/shard_map/reduce_scatter | solution.py:102
  (107 shorter events, 71.3 us)
Async XLA Ops:
  7.2 211.8 %copy-start = (bf16[27,128,512]{2,1,0:T(8,128)(2,1)S(1)}, bf16[27,128,512]{2,1,0:T(8,128)(2,1)}, u32[]{:S(2)}) copy-start(bf16[27,128,512]{2,1,0:T(8,128)(2,1)} %param.5) | copy-start | bytes 10616836
  7.2 202.4 %all-gather.2.cloned.1.call-start = ((), (), s32[]{:S(2)}) async-start(), calls=%async_computation.2 | async-start | bytes 3932160 | tf_op jit(solution)/shard_map/all_gather | solution.py:96
  9.2 3.7 collective-permute-start
  11.6 3.6 collective-permute-start.1
  17.2 317.9 %reduce-scatter.7.cloned.1.call-start = ((), (), s32[]{:S(2)}) async-start(), calls=%async_computation.4 | async-start | bytes 1310720
  17.2 3.4 collective-permute-start.4
  19.3 3.6 collective-permute-start.5
  20.6 2.3 copy-start.11
  24.9 44.9 %collective-permute-start.6 = (bf16[1,128,1,3,1024]{4,1,3,2,0:T(8,128)(2,1)}, bf16[1,128,1,3,1024]{4,1,3,2,0:T(8,128)(2,1)}, u32[]{:S(2)}, u32[]{:S(2)}) collective-permute-start(bf16[1,128,1,3,1024]{4,1,3,2,0:T(8,128)(2,1)} %maximum_bitcast_fusion), channel_id=1, source_target_pairs={{0,2},{2,0},{4,6},{6,4},{1,3},{3,1},{5,7},{7,5},{8,10},{10,8},{12,... | collective-permute-start | bytes 2359304 | tf_op jit(solution)/shard_map/ppermute | solution.py:19
  71.3 2.2 copy-start.5
  73.5 92.2 %collective-permute-start.7 = (bf16[2,128,1,3,1024]{4,1,3,2,0:T(8,128)(2,1)}, bf16[2,128,1,3,1024]{4,1,3,2,0:T(8,128)(2,1)}, u32[]{:S(2)}, u32[]{:S(2)}) collective-permute-start(bf16[2,128,1,3,1024]{4,1,3,2,0:T(8,128)(2,1)} %pad_maximum_fusion.2), channel_id=1, source_target_pairs={{0,4},{2,6},{4,0},{6,2},{1,5},{3,7},{5,1},{7,3},{8,12},{10,14},{12... | collective-permute-start | bytes 4718600 | tf_op jit(solution)/shard_map/ppermute | solution.py:19
  216.3 2.6 copy-start.14
  218.9 15.4 %copy-start.3 = (bf16[512,3,32,1,8,5]{0,4,5,2,1,3:T(8,128)(2,1)S(1)}, bf16[512,3,32,1,8,5]{0,4,5,2,1,3:T(8,128)(2,1)}, u32[]{:S(2)}) copy-start(bf16[512,3,32,1,8,5]{0,4,5,2,1,3:T(8,128)(2,1)} %copy-done.2) | copy-start | bytes 11796484
  218.9 15.4 %copy-start.10 = (bf16[512,3,32,1,7,2]{0,4,5,2,1,3:T(8,128)(2,1)S(1)}, bf16[512,3,32,1,7,2]{0,4,5,2,1,3:T(8,128)(2,1)}, u32[]{:S(2)}) copy-start(bf16[512,3,32,1,7,2]{0,4,5,2,1,3:T(8,128)(2,1)} %slice.20) | copy-start | bytes 4128772
  230.6 51.6 %collective-permute-start.2 = (bf16[128,1,1,1024]{0,3,2,1:T(8,128)(2,1)}, bf16[128,1,1,1024]{0,3,2,1:T(8,128)(2,1)}, u32[]{:S(2)}, u32[]{:S(2)}) collective-permute-start(bf16[128,1,1,1024]{0,3,2,1:T(8,128)(2,1)} %bitcast.41), channel_id=1, source_target_pairs={{0,1},{2,3},{4,5},{6,7},{8,9},{10,11},{12,13},{14,15},{16,17},{18,... | collective-permute-start | bytes 786440 | tf_op jit(solution)/shard_map/ppermute | solution.py:37
  232.9 51.6 %collective-permute-start.3 = (bf16[128,1,1,1024]{0,3,2,1:T(8,128)(2,1)}, bf16[128,1,1,1024]{0,3,2,1:T(8,128)(2,1)}, u32[]{:S(2)}, u32[]{:S(2)}) collective-permute-start(bf16[128,1,1,1024]{0,3,2,1:T(8,128)(2,1)} %bitcast.41), channel_id=1, source_target_pairs={{1,0},{3,2},{5,4},{7,6},{9,8},{11,10},{13,12},{15,14},{17,16},{19,... | collective-permute-start | bytes 786440 | tf_op jit(solution)/shard_map/ppermute | solution.py:38
  245.9 10.3 %copy-start.9 = (bf16[128,1,1,32,32]{0,3,4,1,2:T(8,128)(2,1)}, bf16[128,1,1,32,32]{0,3,4,1,2:T(8,128)(2,1)S(1)}, u32[]{:S(2)}) copy-start(bf16[128,1,1,32,32]{0,3,4,1,2:T(8,128)(2,1)S(1)} %slice_bitcast_fusion.2) | copy-start | bytes 786436
  246.7 40.1 %collective-permute-start.8 = (bf16[128,1,1,1024]{0,3,2,1:T(8,128)(2,1)}, bf16[128,1,1,1024]{0,3,2,1:T(8,128)(2,1)}, u32[]{:S(2)}, u32[]{:S(2)}) collective-permute-start(bf16[128,1,1,1024]{0,3,2,1:T(8,128)(2,1)} %bitcast.20), channel_id=1, source_target_pairs={{0,1},{2,3},{4,5},{6,7},{8,9},{10,11},{12,13},{14,15},{16,17},{18,... | collective-permute-start | bytes 786440 | tf_op jit(solution)/shard_map/ppermute | solution.py:37
  251.1 36.8 %collective-permute-start.9 = (bf16[128,1,1,1024]{0,3,2,1:T(8,128)(2,1)}, bf16[128,1,1,1024]{0,3,2,1:T(8,128)(2,1)}, u32[]{:S(2)}, u32[]{:S(2)}) collective-permute-start(bf16[128,1,1,1024]{0,3,2,1:T(8,128)(2,1)} %bitcast.20), channel_id=1, source_target_pairs={{1,0},{3,2},{5,4},{7,6},{9,8},{11,10},{13,12},{15,14},{17,16},{19,... | collective-permute-start | bytes 786440 | tf_op jit(solution)/shard_map/ppermute | solution.py:38
  295.9 2.1 copy-start.7
  298.0 143.0 %all-reduce.3.cloned.1.call-start = ((), (), s32[]{:S(2)}) async-start(), calls=%async_computation.5 | async-start | bytes 14155776 | tf_op jit(solution)/shard_map/psum | solution.py:125
  323.5 163.4 %reduce-scatter.5.cloned.1.call-start = ((), (), s32[]{:S(2)}) async-start(), calls=%async_computation.3 | async-start | bytes 2621440 | tf_op jit(solution)/shard_map/reduce_scatter | solution.py:102
  440.9 6.1 %copy-start.8 = (bf16[27,128,512]{2,1,0:T(8,128)(2,1)S(1)}, bf16[27,128,512]{2,1,0:T(8,128)(2,1)}, u32[]{:S(2)}) copy-start(bf16[27,128,512]{2,1,0:T(8,128)(2,1)} %get-tuple-element.17) | copy-start | bytes 10616836
  447.0 43.4 %copy-start.1 = (bf16[27,128,512]{2,1,0:T(8,128)(2,1)S(1)}, bf16[27,128,512]{2,1,0:T(8,128)(2,1)}, u32[]{:S(2)}) copy-start(bf16[27,128,512]{2,1,0:T(8,128)(2,1)} %param.5) | copy-start | bytes 10616836
  (6 other events, 9.7 us)
Sparse Core Ops, SparseCore 0:
  17.3 127.1 all-gather.1
  298.1 27.7 reduce-scatter.6
  329.8 111.0 all-reduce.2
  443.1 43.7 reduce-scatter.4
